TPU v7x, 32 devices: a whole 2x2x4 slice. The times are simulated.
32 devices in a mesh: row: 2 (over x), col: 16 (over z, y, core).
Axes of the slice: x: 2, y: 2, z: 4, core: 2. Of those that a mesh axis runs over, the one named last changes fastest.
Arguments:
- query_proj: bfloat16 [16384, 4096], P(('col', 'row')), may hold values from -9 to 9
- key_proj: bfloat16 [16384, 512], P(('col', 'row')), may hold values from -9 to 9
- value_proj: bfloat16 [16384, 512], P(('col', 'row')), may hold values from -6 to 6
- segment_ids: int32 [16, 1024], P('col'), may hold values from 0 to 3, never falling along the last dimension, each value on 1 to 512 neighbouring positions
- out_weight: bfloat16 [4096, 8192], P('col', 'row'), may hold values from -0.09375 to 0.09375
- residual: bfloat16 [16384, 8192], P('col', 'row'), may hold values from -4 to 4
- norm_gain: float32 [8192], P('row'), may hold values from 0.1 to 1.9
Outputs:
- residual_sum: bfloat16 [16384, 8192], P('col', 'row')
- normed: bfloat16 [16384, 8192], P('col', 'row')
Inputs may be any that keep to these rules, and one draw needn't show every extreme that they name: `segment_ids`: along each packed sequence the document number never falls; each document spans at most 512 positions and one spans exactly that.
All inputs are finite; a program needn't handle non-finite values.
Results may differ from a plain program's by a relative error of at most 0.0044.
Values may be sent and summed in bfloat16 or wider, within the bound.
A program may use at most 192 MiB of HBM per device.

v0:
```python
import jax
import jax.numpy as jnp
from jax import lax
from jax.sharding import PartitionSpec as P

D = 8192
HD = 128
HK = 4


def attend_local(query_heads, key_heads, value_heads, segment_row):
    length = query_heads.shape[0]
    kv_local = key_heads.shape[1] // HD
    group = query_heads.shape[1] // HD // kv_local
    query_grid = query_heads.reshape(length, kv_local, group, HD).transpose(1, 2, 0, 3)
    key_grid = key_heads.reshape(length, kv_local, HD).transpose(1, 0, 2)
    value_grid = value_heads.reshape(length, kv_local, HD).transpose(1, 0, 2)
    places = jnp.arange(length)
    allowed = (segment_row[:, None] == segment_row[None, :]) & (places[None, :] <= places[:, None])

    def one_group(operands):
        group_query, group_key, group_value = operands
        scores = jnp.einsum(
            "gqd,kd->gqk", group_query, group_key, preferred_element_type=jnp.float32
        ) * HD ** (-0.5)
        scores = jnp.where(allowed, scores, jnp.float32(-1e30))
        peak = jnp.max(scores, axis=-1, keepdims=True)
        weights = jnp.where(allowed, jnp.exp(scores - peak), jnp.float32(0.0))
        totals = jnp.sum(weights, axis=-1, keepdims=True)
        probs = weights.astype(jnp.bfloat16)
        mixture = (
            jnp.einsum("gqk,kd->gqd", probs, group_value, preferred_element_type=jnp.float32)
            / totals
        )
        return mixture.astype(jnp.bfloat16)

    heads_out = lax.map(one_group, (query_grid, key_grid, value_grid))
    return heads_out.transpose(2, 0, 1, 3).reshape(length, kv_local * group * HD)


def widen_heads(proj_rows, repeat):
    rows_local = proj_rows.shape[0]
    kv_count = proj_rows.shape[1] // HD
    if repeat == 1:
        return proj_rows
    spread = jnp.broadcast_to(
        proj_rows.reshape(rows_local, kv_count, 1, HD), (rows_local, kv_count, repeat, HD)
    )
    return spread.reshape(rows_local, kv_count * repeat * HD)


def body(query_proj, key_proj, value_proj, segment_ids, out_weight, residual, norm_gain):
    row_count = lax.axis_size("row")
    repeat = max(row_count // HK, 1)
    key_wide = widen_heads(key_proj, repeat)
    value_wide = widen_heads(value_proj, repeat)
    query_heads, key_heads, value_heads = (
        lax.all_to_all(query_proj, "row", split_axis=1, concat_axis=0, tiled=True),
        lax.all_to_all(key_wide, "row", split_axis=1, concat_axis=0, tiled=True),
        lax.all_to_all(value_wide, "row", split_axis=1, concat_axis=0, tiled=True),
    )
    attn = attend_local(query_heads, key_heads, value_heads, segment_ids[0])
    panel_rows = lax.all_gather(attn, "row", axis=1, tiled=True)
    projected = jnp.dot(
        panel_rows,
        lax.all_gather(out_weight, "col", axis=0, tiled=True),
        preferred_element_type=jnp.float32,
    )
    hidden_sum = residual.astype(jnp.float32) + projected
    squares = lax.psum(jnp.sum(hidden_sum * hidden_sum, axis=1), "row")
    scaled = lax.rsqrt(squares / D + jnp.float32(1e-05))
    normed = hidden_sum * scaled[:, None] * norm_gain[None, :]
    return (hidden_sum.astype(jnp.bfloat16), normed.astype(jnp.bfloat16))


def solution(mesh):
    placed = (
        P(("col", "row"), None),
        P(("col", "row"), None),
        P(("col", "row"), None),
        P("col", None),
        P("col", "row"),
        P("col", "row"),
        P("row"),
    )
    return jax.shard_map(
        body,
        mesh=mesh,
        in_specs=placed,
        out_specs=(P("col", "row"), P("col", "row")),
        check_vma=False,
    )
```

profile of v0, /device:TPU:0, one launch (start us, length us, event | category | flops | bytes accessed | tf_op | source)
XLA Modules:
  0.0 514.9 jit_solution(6233350073334996084)
XLA Ops:
  7.2 1.9 copy.42
  9.0 4.2 all-to-all-start.1
  13.2 1.9 copy.41
  15.1 6.9 %all-to-all-done.1 = bf16[512,2,256]{2,0,1:T(8,128)(2,1)S(1)} async-done(((bf16[512,2,256]{2,0,1:T(8,128)(2,1)}), bf16[512,2,256]{2,0,1:T(8,128)(2,1)S(1)}, u32[]{:S(2)}, u32[]{:S(2)}) %all-to-all-start.1) | async-done | bytes 524320 | tf_op jit(solution)/shard_map/all_to_all | solution.py:59
  22.0 3.5 all-to-all-start.2
  25.5 4.8 copy.40
  30.3 2.9 all-to-all-done.2
  33.1 5.6 %all-to-all-start = ((bf16[512,2,2048]{2,0,1:T(8,128)(2,1)}), bf16[512,2,2048]{2,0,1:T(8,128)(2,1)}, u32[]{:S(2)}, u32[]{:S(2)}) async-start(bf16[512,2,2048]{2,0,1:T(8,128)(2,1)} %bitcast.71), calls=%async_computation | async-start | bytes 8388608 | tf_op jit(solution)/shard_map/all_to_all | solution.py:58
  38.8 0.1 reshape.34
  39.0 0.9 copy.15
  40.0 0.9 copy.16
  40.9 44.1 %all-to-all-done = bf16[512,2,2048]{2,0,1:T(8,128)(2,1)} async-done(((bf16[512,2,2048]{2,0,1:T(8,128)(2,1)}), bf16[512,2,2048]{2,0,1:T(8,128)(2,1)}, u32[]{:S(2)}, u32[]{:S(2)}) %all-to-all-start) | async-done | bytes 4194336 | tf_op jit(solution)/shard_map/all_to_all | solution.py:58
  85.0 5.6 %copy.25 = bf16[128,8,16,128]{3,2,1,0:T(8,128)(2,1)} copy(bf16[128,8,16,128]{3,1,2,0:T(8,128)(2,1)} %bitcast.23) | data formatting | bytes 8388608
  90.6 74.1 %while.11 = (s32[]{:T(128)}, bf16[2,8,1024,128]{2,3,1,0:T(8,128)(2,1)}, bf16[2,8,1024,128]{3,1,0,2:T(8,128)(2,1)}, bf16[2,1024,128]{2,1,0:T(8,128)(2,1)}, bf16[2...) while((s32[]{:T(128)}, bf16[2,8,1024,128]{2,3,1,0:T(8,128)(2,1)}, ...), condition=%wide.region_3.4_spmd.clone, body=%wide.region_0.3_spmd.clone.sunk | while | flops 4350542848 | bytes 54072912 | solution.py:37
  90.6 1.7 constant_dynamic-slice_fusion.2
  92.3 0.6 fusion.52
  92.9 20.1 %fusion.53 = (f32[8,1024]{1,0:T(8,128)S(1)}, bf16[8,1024,1024]{1,2,0:T(8,128)(2,1)}) fusion(pred[1024,1024]{0,1:T(8,128)(4,1)S(1)} %fusion.52, bf16[1,8,1024,128]{3,1,0,2:T(8,128)(2,1)S(1)} %constant_dynamic-slice_fusion.2, bf16[2,1024,128]{2,1,0:T(8,128)(2,1)} %get-tuple-element.134, s32[]{:T(128)} %get-tuple-element.124), kind=kOutput, calls=%fused_computation.37.clone.1 | convolution fusion | flops 2197816320 | bytes 21266944 | tf_op jit(solution)/shard_map/while/body/eval_jaxpr/sub | solution.py:28
  113.1 10.1 %fusion.54 = bf16[1,8,1024,128]{3,2,1,0:T(8,128)(2,1)} fusion(f32[8,1024]{1,0:T(8,128)S(1)} %get-tuple-element.115, bf16[8,1024,1024]{1,2,0:T(8,128)(2,1)} %get-tuple-element.116, bf16[2,1024,128]{2,1,0:T(8,128)(2,1)} %get-tuple-element.135, s32[]{:T(128)} %get-tuple-element.124), kind=kOutput, calls=%fused_computation.16.clone.1 | convolution fusion | flops 2149580800 | bytes 19169792 | tf_op jit(solution)/shard_map/while/body/eval_jaxpr/gqk,kd->gqd/dot_general | solution.py:32
  123.2 2.9 copy.46
  126.0 1.6 constant_dynamic-update-slice_fusion.2
  127.6 1.7 constant_dynamic-slice_fusion.2
  129.4 0.6 fusion.52
  130.0 20.1 %fusion.53 = (f32[8,1024]{1,0:T(8,128)S(1)}, bf16[8,1024,1024]{1,2,0:T(8,128)(2,1)}) fusion(pred[1024,1024]{0,1:T(8,128)(4,1)S(1)} %fusion.52, bf16[1,8,1024,128]{3,1,0,2:T(8,128)(2,1)S(1)} %constant_dynamic-slice_fusion.2, bf16[2,1024,128]{2,1,0:T(8,128)(2,1)} %get-tuple-element.134, s32[]{:T(128)} %get-tuple-element.124), kind=kOutput, calls=%fused_computation.37.clone.1 | convolution fusion | flops 2197816320 | bytes 21266944 | tf_op jit(solution)/shard_map/while/body/eval_jaxpr/sub | solution.py:28
  150.1 10.1 %fusion.54 = bf16[1,8,1024,128]{3,2,1,0:T(8,128)(2,1)} fusion(f32[8,1024]{1,0:T(8,128)S(1)} %get-tuple-element.115, bf16[8,1024,1024]{1,2,0:T(8,128)(2,1)} %get-tuple-element.116, bf16[2,1024,128]{2,1,0:T(8,128)(2,1)} %get-tuple-element.135, s32[]{:T(128)} %get-tuple-element.124), kind=kOutput, calls=%fused_computation.16.clone.1 | convolution fusion | flops 2149580800 | bytes 19169792 | tf_op jit(solution)/shard_map/while/body/eval_jaxpr/gqk,kd->gqd/dot_general | solution.py:32
  160.2 2.9 copy.46
  163.1 1.6 constant_dynamic-update-slice_fusion.2
  164.8 0.7 all-gather.5.cloned.1.call-update
  165.5 103.3 %all-gather.3.cloned.1.call-done = bf16[1024,4096]{0,1:T(8,128)(2,1)} async-done(((bf16[1024,2048]{0,1:T(8,128)(2,1)}), bf16[1024,4096]{0,1:T(8,128)(2,1)}) %all-gather.3.cloned.1.call-update) | async-done | bytes 8388624 | tf_op jit(solution)/shard_map/all_gather | solution.py:63
  268.8 169.7 %all-gather.5.cloned.1.call-done = bf16[4096,4096]{1,0:T(8,128)(2,1)} async-done(((bf16[256,4096]{1,0:T(8,128)(2,1)}), bf16[4096,4096]{1,0:T(8,128)(2,1)}) %all-gather.5.cloned.1.call-update) | async-done | bytes 33554448 | tf_op jit(solution)/shard_map/all_gather | solution.py:66
  438.5 45.1 %multiply_reduce_fusion = (f32[1024]{0:T(1024)S(1)}, f32[1024,4096]{1,0:T(8,128)}) fusion(bf16[1024,4096]{0,1:T(8,128)(2,1)} %all-gather.3.cloned.1.call-done, bf16[4096,4096]{1,0:T(8,128)(2,1)} %all-gather.5.cloned.1.call-done, bf16[1024,4096]{1,0:T(8,128)(2,1)} %param.14), kind=kOutput, calls=%fused_computation.31 | convolution fusion | flops 34376515584 | bytes 67112960 | tf_op jit(solution)/shard_map/dot_general | solution.py:64
  483.6 4.9 psum.7
  488.5 19.5 %multiply_convert_fusion = (bf16[1024,4096]{1,0:T(8,128)(2,1)}, bf16[1024,4096]{1,0:T(8,128)(2,1)}) fusion(f32[1024,4096]{1,0:T(8,128)} %get-tuple-element.73, f32[4096]{0:T(1024)S(1)} %copy-done.1, f32[1024]{0:T(1024)S(1)} %add_rsqrt_fusion), kind=kLoop, calls=%fused_computation.30 | loop fusion | flops 16777216 | bytes 33574912 | tf_op jit(solution)/shard_map/convert_element_type | solution.py:73
  (10 shorter events, 0.2 us)
Async XLA Ops:
  9.0 12.9 %all-to-all-start.1 = ((bf16[512,2,256]{2,0,1:T(8,128)(2,1)}), bf16[512,2,256]{2,0,1:T(8,128)(2,1)S(1)}, u32[]{:S(2)}, u32[]{:S(2)}) async-start(bf16[512,2,256]{2,0,1:T(8,128)(2,1)} %bitcast.59), calls=%async_computation.1 | async-start | bytes 1048576 | tf_op jit(solution)/shard_map/all_to_all | solution.py:59
  22.0 11.2 %all-to-all-start.2 = ((bf16[512,2,256]{2,0,1:T(8,128)(2,1)}), bf16[512,2,256]{2,0,1:T(8,128)(2,1)S(1)}, u32[]{:S(2)}, u32[]{:S(2)}) async-start(bf16[512,2,256]{2,0,1:T(8,128)(2,1)} %bitcast.58), calls=%async_computation.2 | async-start | bytes 1048576 | tf_op jit(solution)/shard_map/all_to_all | solution.py:60
  33.1 51.8 %all-to-all-start = ((bf16[512,2,2048]{2,0,1:T(8,128)(2,1)}), bf16[512,2,2048]{2,0,1:T(8,128)(2,1)}, u32[]{:S(2)}, u32[]{:S(2)}) async-start(bf16[512,2,2048]{2,0,1:T(8,128)(2,1)} %bitcast.71), calls=%async_computation | async-start | bytes 8388608 | tf_op jit(solution)/shard_map/all_to_all | solution.py:58
  38.8 51.8 %copy-start = (s32[1,1024]{1,0:T(1,128)S(1)}, s32[1,1024]{1,0:T(1,128)}, u32[]{:S(2)}) copy-start(s32[1,1024]{1,0:T(1,128)} %param.12) | copy-start | bytes 12292
  38.8 230.0 %all-gather.3.cloned.1.call-start = ((), (), s32[]{:S(2)}) async-start(), calls=%async_computation.3 | async-start | bytes 12582912 | tf_op jit(solution)/shard_map/all_gather | solution.py:63
  164.7 273.8 %all-gather.5.cloned.1.call-start = ((), (), s32[]{:S(2)}) async-start(), calls=%async_computation.4 | async-start | bytes 35651584 | tf_op jit(solution)/shard_map/all_gather | solution.py:66
  165.5 323.1 %copy-start.1 = (f32[4096]{0:T(1024)S(1)}, f32[4096]{0:T(1024)}, u32[]{:S(2)}) copy-start(f32[4096]{0:T(1024)} %param.15) | copy-start | bytes 49156
Sparse Core Ops, SparseCore 0:
  164.9 103.9 all-gather.2
  270.4 168.0 all-gather.4
where the time goes:
time: 516 us; the launch traced here: 515 us
  waiting for transfers between devices  328 us (64%)
  matrix products  106 us (21%)
  local copies, waits for them, and re-layouts  28.5 us (6%)
  other arithmetic  20.7 us (4%)
  between operations  14.1 us (3%)
  starting transfers between devices  13.4 us (3%)
    all_gather x1, waiting for transfers between devices, body(): lax.all_gather(out_weight, 'col', axis=0, tiled=True)  170 us
    all_gather x1, waiting for transfers between devices, body(): panel_rows = lax.all_gather(attn, 'row', axis=1, tiled=True)  103 us
    dot_general x1, matrix products, body(): jnp.dot(panel_rows, lax.all_gather(out_weight, 'col', axis=0, tiled=True)...  45.1 us
    all_to_all x1, waiting for transfers between devices, body(): lax.all_to_all(query_proj, 'row', split_axis=1, concat_axis=0, tiled=True)  44.1 us
    sub x2, matrix products, one_group(): weights = jnp.where(allowed, jnp.exp(scores - peak), jnp.float32(0.0))  40.3 us
    dot_general x2, matrix products, one_group(): jnp.einsum('gqk,kd->gqd', probs, group_value, preferred_element_type=jnp....  20.2 us
    convert_element_type x1, other arithmetic, body(): return (hidden_sum.astype(jnp.bfloat16), normed.astype(jnp.bfloat16))  19.5 us
  transfers between devices with their start and end apart: 5, of which 5 were waited for; matrix products, arithmetic and copies ran while one was open for 2% of the time, Pallas kernels for 0%

commit v1 on v0

--- a/solution.py
+++ b/solution.py
@@ -6,6 +6,15 @@
 D = 8192
 HD = 128
 HK = 4
+play_the_rates = lambda join_dim, row_data, at_axis: jnp.concatenate(
+    lax.all_to_all(
+        jnp.stack(jnp.split(row_data, lax.axis_size("row"), join_dim), 0),
+        axis_name="row",
+        split_axis=0,
+        concat_axis=0,
+    ),
+    at_axis,
+)
 
 
 def attend_local(query_heads, key_heads, value_heads, segment_row):
@@ -56,7 +65,7 @@
     value_wide = widen_heads(value_proj, repeat)
     query_heads, key_heads, value_heads = (
         lax.all_to_all(query_proj, "row", split_axis=1, concat_axis=0, tiled=True),
-        lax.all_to_all(key_wide, "row", split_axis=1, concat_axis=0, tiled=True),
+        play_the_rates(1, row_data=key_wide, at_axis=0),
         lax.all_to_all(value_wide, "row", split_axis=1, concat_axis=0, tiled=True),
     )
     attn = attend_local(query_heads, key_heads, value_heads, segment_ids[0])

time: 516 us -> 516 us (level)
  no operation moved by 1% of the time
where the time goes in v1:
time: 516 us; the launch traced here: 515 us
  waiting for transfers between devices  328 us (64%)
  matrix products  106 us (21%)
  local copies, waits for them, and re-layouts  27.7 us (5%)
  other arithmetic  21.6 us (4%)
  between operations  14.1 us (3%)
  starting transfers between devices  13.4 us (3%)
    all_gather x1, waiting for transfers between devices, body(): lax.all_gather(out_weight, 'col', axis=0, tiled=True)  170 us
    all_gather x1, waiting for transfers between devices, body(): panel_rows = lax.all_gather(attn, 'row', axis=1, tiled=True)  103 us
    dot_general x1, matrix products, body(): jnp.dot(panel_rows, lax.all_gather(out_weight, 'col', axis=0, tiled=True)...  45 us
    all_to_all x1, waiting for transfers between devices, body(): lax.all_to_all(query_proj, 'row', split_axis=1, concat_axis=0, tiled=True)  44.1 us
    sub x2, matrix products, one_group(): weights = jnp.where(allowed, jnp.exp(scores - peak), jnp.float32(0.0))  40.3 us
    dot_general x2, matrix products, one_group(): jnp.einsum('gqk,kd->gqd', probs, group_value, preferred_element_type=jnp....  20.2 us
    convert_element_type x1, other arithmetic, body(): return (hidden_sum.astype(jnp.bfloat16), normed.astype(jnp.bfloat16))  19.6 us
  transfers between devices with their start and end apart: 5, of which 5 were waited for; matrix products, arithmetic and copies ran while one was open for 2% of the time, Pallas kernels for 0%

profile of v1, /device:TPU:0, one launch (start us, length us, event | category | flops | bytes accessed | tf_op | source)
XLA Modules:
  0.0 515.0 jit_solution(9314845042968437290)
XLA Ops:
  7.2 1.1 slice_bitcast_fusion.1
  8.2 0.8 pad_maximum_fusion
  9.1 4.2 all-to-all-start.1
  13.3 1.9 copy.38
  15.1 6.9 %all-to-all-done.1 = bf16[2,512,256]{2,1,0:T(8,128)(2,1)S(1)} async-done(((bf16[2,512,256]{2,1,0:T(8,128)(2,1)}), bf16[2,512,256]{2,1,0:T(8,128)(2,1)S(1)}, u32[]{:S(2)}, u32[]{:S(2)}) %all-to-all-start.1) | async-done | bytes 524320 | tf_op jit(solution)/shard_map/all_to_all | solution.py:10
  22.0 3.5 all-to-all-start.2
  25.5 4.8 copy.37
  30.3 2.9 all-to-all-done.2
  33.2 5.6 %all-to-all-start = ((bf16[512,2,2048]{2,0,1:T(8,128)(2,1)}), bf16[512,2,2048]{2,0,1:T(8,128)(2,1)}, u32[]{:S(2)}, u32[]{:S(2)}) async-start(bf16[512,2,2048]{2,0,1:T(8,128)(2,1)} %bitcast.70), calls=%async_computation | async-start | bytes 8388608 | tf_op jit(solution)/shard_map/all_to_all | solution.py:67
  39.0 0.9 copy.14
  40.0 0.9 copy.15
  40.9 44.1 %all-to-all-done = bf16[512,2,2048]{2,0,1:T(8,128)(2,1)} async-done(((bf16[512,2,2048]{2,0,1:T(8,128)(2,1)}), bf16[512,2,2048]{2,0,1:T(8,128)(2,1)}, u32[]{:S(2)}, u32[]{:S(2)}) %all-to-all-start) | async-done | bytes 4194336 | tf_op jit(solution)/shard_map/all_to_all | solution.py:67
  85.0 5.6 %copy.23 = bf16[128,8,16,128]{3,2,1,0:T(8,128)(2,1)} copy(bf16[128,8,16,128]{3,1,2,0:T(8,128)(2,1)} %bitcast.22) | data formatting | bytes 8388608
  90.6 74.1 %while.11 = (s32[]{:T(128)}, bf16[2,8,1024,128]{2,3,1,0:T(8,128)(2,1)}, bf16[2,8,1024,128]{3,1,0,2:T(8,128)(2,1)}, bf16[2,1024,128]{2,1,0:T(8,128)(2,1)}, bf16[2...) while((s32[]{:T(128)}, bf16[2,8,1024,128]{2,3,1,0:T(8,128)(2,1)}, ...), condition=%wide.region_3.4_spmd.clone, body=%wide.region_0.3_spmd.clone.sunk | while | flops 4350542848 | bytes 54072912 | solution.py:46
  90.6 1.7 constant_dynamic-slice_fusion.2
  92.4 0.6 fusion.52
  93.0 20.1 %fusion.53 = (f32[8,1024]{1,0:T(8,128)S(1)}, bf16[8,1024,1024]{1,2,0:T(8,128)(2,1)}) fusion(pred[1024,1024]{0,1:T(8,128)(4,1)S(1)} %fusion.52, bf16[1,8,1024,128]{3,1,0,2:T(8,128)(2,1)S(1)} %constant_dynamic-slice_fusion.2, bf16[2,1024,128]{2,1,0:T(8,128)(2,1)} %get-tuple-element.136, s32[]{:T(128)} %get-tuple-element.126), kind=kOutput, calls=%fused_computation.39.clone.1 | convolution fusion | flops 2197816320 | bytes 21266944 | tf_op jit(solution)/shard_map/while/body/eval_jaxpr/sub | solution.py:37
  113.1 10.1 %fusion.54 = bf16[1,8,1024,128]{3,2,1,0:T(8,128)(2,1)} fusion(f32[8,1024]{1,0:T(8,128)S(1)} %get-tuple-element.117, bf16[8,1024,1024]{1,2,0:T(8,128)(2,1)} %get-tuple-element.118, bf16[2,1024,128]{2,1,0:T(8,128)(2,1)} %get-tuple-element.137, s32[]{:T(128)} %get-tuple-element.126), kind=kOutput, calls=%fused_computation.16.clone.1 | convolution fusion | flops 2149580800 | bytes 19169792 | tf_op jit(solution)/shard_map/while/body/eval_jaxpr/gqk,kd->gqd/dot_general | solution.py:41
  123.2 2.9 copy.42
  126.1 1.6 constant_dynamic-update-slice_fusion.2
  127.7 1.7 constant_dynamic-slice_fusion.2
  129.4 0.6 fusion.52
  130.0 20.2 %fusion.53 = (f32[8,1024]{1,0:T(8,128)S(1)}, bf16[8,1024,1024]{1,2,0:T(8,128)(2,1)}) fusion(pred[1024,1024]{0,1:T(8,128)(4,1)S(1)} %fusion.52, bf16[1,8,1024,128]{3,1,0,2:T(8,128)(2,1)S(1)} %constant_dynamic-slice_fusion.2, bf16[2,1024,128]{2,1,0:T(8,128)(2,1)} %get-tuple-element.136, s32[]{:T(128)} %get-tuple-element.126), kind=kOutput, calls=%fused_computation.39.clone.1 | convolution fusion | flops 2197816320 | bytes 21266944 | tf_op jit(solution)/shard_map/while/body/eval_jaxpr/sub | solution.py:37
  150.2 10.1 %fusion.54 = bf16[1,8,1024,128]{3,2,1,0:T(8,128)(2,1)} fusion(f32[8,1024]{1,0:T(8,128)S(1)} %get-tuple-element.117, bf16[8,1024,1024]{1,2,0:T(8,128)(2,1)} %get-tuple-element.118, bf16[2,1024,128]{2,1,0:T(8,128)(2,1)} %get-tuple-element.137, s32[]{:T(128)} %get-tuple-element.126), kind=kOutput, calls=%fused_computation.16.clone.1 | convolution fusion | flops 2149580800 | bytes 19169792 | tf_op jit(solution)/shard_map/while/body/eval_jaxpr/gqk,kd->gqd/dot_general | solution.py:41
  160.3 2.9 copy.42
  163.1 1.6 constant_dynamic-update-slice_fusion.2
  164.8 0.7 all-gather.5.cloned.1.call-update
  165.5 103.3 %all-gather.3.cloned.1.call-done = bf16[1024,4096]{0,1:T(8,128)(2,1)} async-done(((bf16[1024,2048]{0,1:T(8,128)(2,1)}), bf16[1024,4096]{0,1:T(8,128)(2,1)}) %all-gather.3.cloned.1.call-update) | async-done | bytes 8388624 | tf_op jit(solution)/shard_map/all_gather | solution.py:72
  268.9 169.7 %all-gather.5.cloned.1.call-done = bf16[4096,4096]{1,0:T(8,128)(2,1)} async-done(((bf16[256,4096]{1,0:T(8,128)(2,1)}), bf16[4096,4096]{1,0:T(8,128)(2,1)}) %all-gather.5.cloned.1.call-update) | async-done | bytes 33554448 | tf_op jit(solution)/shard_map/all_gather | solution.py:75
  438.6 45.0 %multiply_reduce_fusion = (f32[1024]{0:T(1024)S(1)}, f32[1024,4096]{1,0:T(8,128)}) fusion(bf16[1024,4096]{0,1:T(8,128)(2,1)} %all-gather.3.cloned.1.call-done, bf16[4096,4096]{1,0:T(8,128)(2,1)} %all-gather.5.cloned.1.call-done, bf16[1024,4096]{1,0:T(8,128)(2,1)} %param.14), kind=kOutput, calls=%fused_computation.31 | convolution fusion | flops 34376515584 | bytes 67112960 | tf_op jit(solution)/shard_map/dot_general | solution.py:73
  483.6 4.9 psum.7
  488.5 19.6 %multiply_convert_fusion = (bf16[1024,4096]{1,0:T(8,128)(2,1)}, bf16[1024,4096]{1,0:T(8,128)(2,1)}) fusion(f32[1024,4096]{1,0:T(8,128)} %get-tuple-element.75, f32[4096]{0:T(1024)S(1)} %copy-done.1, f32[1024]{0:T(1024)S(1)} %add_rsqrt_fusion), kind=kLoop, calls=%fused_computation.30 | loop fusion | flops 16777216 | bytes 33574912 | tf_op jit(solution)/shard_map/convert_element_type | solution.py:82
  (11 shorter events, 0.4 us)
Async XLA Ops:
  9.1 12.9 %all-to-all-start.1 = ((bf16[2,512,256]{2,1,0:T(8,128)(2,1)}), bf16[2,512,256]{2,1,0:T(8,128)(2,1)S(1)}, u32[]{:S(2)}, u32[]{:S(2)}) async-start(bf16[2,512,256]{2,1,0:T(8,128)(2,1)} %pad_maximum_fusion), calls=%async_computation.1 | async-start | bytes 1048576 | tf_op jit(solution)/shard_map/all_to_all | solution.py:10
  22.0 11.2 %all-to-all-start.2 = ((bf16[512,2,256]{2,0,1:T(8,128)(2,1)}), bf16[512,2,256]{2,0,1:T(8,128)(2,1)S(1)}, u32[]{:S(2)}, u32[]{:S(2)}) async-start(bf16[512,2,256]{2,0,1:T(8,128)(2,1)} %bitcast.58), calls=%async_computation.2 | async-start | bytes 1048576 | tf_op jit(solution)/shard_map/all_to_all | solution.py:69
  33.2 51.8 %all-to-all-start = ((bf16[512,2,2048]{2,0,1:T(8,128)(2,1)}), bf16[512,2,2048]{2,0,1:T(8,128)(2,1)}, u32[]{:S(2)}, u32[]{:S(2)}) async-start(bf16[512,2,2048]{2,0,1:T(8,128)(2,1)} %bitcast.70), calls=%async_computation | async-start | bytes 8388608 | tf_op jit(solution)/shard_map/all_to_all | solution.py:67
  38.8 51.8 %copy-start = (s32[1,1024]{1,0:T(1,128)S(1)}, s32[1,1024]{1,0:T(1,128)}, u32[]{:S(2)}) copy-start(s32[1,1024]{1,0:T(1,128)} %param.12) | copy-start | bytes 12292
  38.8 230.1 %all-gather.3.cloned.1.call-start = ((), (), s32[]{:S(2)}) async-start(), calls=%async_computation.3 | async-start | bytes 12582912 | tf_op jit(solution)/shard_map/all_gather | solution.py:72
  164.8 273.8 %all-gather.5.cloned.1.call-start = ((), (), s32[]{:S(2)}) async-start(), calls=%async_computation.4 | async-start | bytes 35651584 | tf_op jit(solution)/shard_map/all_gather | solution.py:75
  165.5 323.0 %copy-start.1 = (f32[4096]{0:T(1024)S(1)}, f32[4096]{0:T(1024)}, u32[]{:S(2)}) copy-start(f32[4096]{0:T(1024)} %param.15) | copy-start | bytes 49156
Sparse Core Ops, SparseCore 0:
  164.9 103.9 all-gather.2
  270.5 168.0 all-gather.4
